TPU v7x, 512 devices: a whole 4x4x16 slice. The times are simulated.
512 devices in a mesh: dp: 16 (over x, y), expert: 32 (over z, core).
Axes of the slice: x: 4, y: 4, z: 16, core: 2. Of those that a mesh axis runs over, the one named last changes fastest.
Arguments:
- tokens: bfloat16 [65536, 3584], P(('dp', 'expert')), may hold values from -6 to 6
- cotangent: bfloat16 [65536, 3584], P(('dp', 'expert')), may hold values from -6 to 6
- route_weight: float32 [65536, 8], P(('dp', 'expert')), may hold values from 0.05 to 0.5
- expert_ids: int32 [65536, 8], P(('dp', 'expert')), may hold values from 0 to 255, as said below
- live_tokens: int32 [512], P(('dp', 'expert')), may hold values from 1 to 128, 49152 in all
- replica_plan: int32 [512, 4], P(('dp', 'expert')), may hold values 0 or 1
- w_gate: bfloat16 [3584, 8192], P('dp', 'expert'), may hold values from -0.09375 to 0.09375
- w_up: bfloat16 [3584, 8192], P('dp', 'expert'), may hold values from -0.09375 to 0.09375
- w_down: bfloat16 [8192, 3584], P('expert', 'dp'), may hold values from -0.125 to 0.125
- scale_gate: float32 [28, 64], P(None, 'expert'), may hold values from 0.5 to 2
- scale_up: float32 [28, 64], P(None, 'expert'), may hold values from 0.5 to 2
- scale_down: float32 [64, 28], P('expert'), may hold values from 0.5 to 2
Outputs:
- d_tokens: bfloat16 [65536, 3584], P(('dp', 'expert'))
- grad_gate: bfloat16 [3584, 8192], P('dp', 'expert')
- grad_up: bfloat16 [3584, 8192], P('dp', 'expert')
- grad_down: bfloat16 [8192, 3584], P('expert', 'dp')
Inputs may be any that keep to these rules, and one draw needn't show every extreme that they name: `expert_ids`: the 8 ids of one token are distinct.
All inputs are finite; a program needn't handle non-finite values. No bound on the sum of `live_tokens` or of `replica_plan` on one device may be relied on, other than what follows from the above.
Results may differ from a plain program's by a relative error of at most 0.012.
Values may be sent and summed in bfloat16 or wider, within the bound.
A program may use at most 64 MiB of HBM per device.

v0:
```python
import jax
import jax.numpy as jnp
from jax import lax
from jax.sharding import PartitionSpec as P

HSH = 8
CAP = 4


def dequantize(values, scale):
    block_rows = values.shape[0] // scale.shape[0]
    block_cols = values.shape[1] // scale.shape[1]
    spread = jnp.repeat(jnp.repeat(scale, block_rows, axis=0), block_cols, axis=1)
    return (values.astype(jnp.float32) * spread).astype(jnp.bfloat16)


def route_rows(tokens, cotangent, route_weight, expert_ids, live_count, plan, experts, capacity):
    count = tokens.shape[0]
    token_index = jnp.arange(count, dtype=jnp.int32)
    expert_index = jnp.arange(experts, dtype=jnp.int32)
    matches = expert_ids[:, None, :] == expert_index[None, :, None]
    routed = jnp.any(matches, axis=2) & (token_index < live_count)[:, None]
    to_replica = (token_index % 2 == 1)[:, None] & (plan[None, :] == 1)
    in_lists = jnp.stack([routed & ~to_replica, routed & to_replica], axis=2).astype(jnp.int32)
    position = jnp.cumsum(in_lists, axis=0) - 1
    capacity_index = jnp.arange(capacity, dtype=jnp.int32)
    selected = ((in_lists[..., None] == 1) & (position[..., None] == capacity_index)).astype(
        jnp.float32
    )
    weight_sum = jnp.sum(jnp.where(matches, route_weight[:, None, :], jnp.float32(0.0)), axis=2)
    row_weight = jnp.sum(selected * weight_sum[:, :, None, None], axis=0)
    flat = selected.reshape(count, -1)
    picker = flat.T.astype(jnp.bfloat16)
    token_rows = jnp.dot(picker, tokens, preferred_element_type=jnp.float32).astype(jnp.bfloat16)
    cot_picked = jnp.dot(picker, cotangent, preferred_element_type=jnp.float32)
    cot_rows = (row_weight.reshape(-1, 1) * cot_picked).astype(jnp.bfloat16)
    shape = (experts, 2, capacity, tokens.shape[1])
    return (flat, token_rows.reshape(shape), cot_rows.reshape(shape))


def expert_terms(token_rows, cot_rows, gate_w, up_w, down_w):
    by_hidden = (((1,), (1,)), ((), ()))
    by_rows = (((0,), (0,)), ((), ()))
    gate_pre = jnp.dot(token_rows, gate_w, preferred_element_type=jnp.float32)
    up_pre = jnp.dot(token_rows, up_w, preferred_element_type=jnp.float32)
    gate_sig = jax.nn.sigmoid(gate_pre)
    swish = gate_pre * gate_sig
    d_hidden = lax.dot_general(cot_rows, down_w, by_hidden, preferred_element_type=jnp.float32)
    hidden = (swish * up_pre).astype(jnp.bfloat16)
    d_up = (d_hidden * swish).astype(jnp.bfloat16)
    d_gate = (d_hidden * up_pre * gate_sig * (1.0 + gate_pre * (1.0 - gate_sig))).astype(
        jnp.bfloat16
    )
    grad_g = lax.dot_general(
        token_rows, d_gate, by_rows, preferred_element_type=jnp.float32
    ).astype(jnp.bfloat16)
    grad_u = lax.dot_general(token_rows, d_up, by_rows, preferred_element_type=jnp.float32).astype(
        jnp.bfloat16
    )
    grad_d = lax.dot_general(cot_rows, hidden, by_rows, preferred_element_type=jnp.float32).astype(
        jnp.bfloat16
    )
    dx_part = lax.dot_general(d_gate, gate_w, by_hidden, preferred_element_type=jnp.float32)
    dx_part = dx_part + lax.dot_general(d_up, up_w, by_hidden, preferred_element_type=jnp.float32)
    return (grad_g, grad_u, grad_d, dx_part.astype(jnp.bfloat16))


def fan_out(rows, members):
    slot_count = rows.shape[0]
    spread = jnp.broadcast_to(rows[:, None], (slot_count, members // slot_count) + rows.shape[1:])
    return spread.reshape((members,) + rows.shape[1:])


def send_rows(token_rows, cot_rows, members):
    return (
        lax.all_to_all(
            fan_out(token_rows, members), "expert", split_axis=0, concat_axis=0, tiled=True
        ),
        lax.all_to_all(
            fan_out(cot_rows, members), "expert", split_axis=0, concat_axis=0, tiled=True
        ),
    )


def on_device(
    tokens,
    cotangent,
    route_weight,
    expert_ids,
    live_tokens,
    replica_plan,
    w_gate,
    w_up,
    w_down,
    scale_gate,
    scale_up,
    scale_down,
):
    members = lax.axis_size("expert")
    groups = lax.axis_size("dp")
    slot_count = members // HSH
    width = tokens.shape[1]
    flat, token_rows, cot_rows = route_rows(
        tokens,
        cotangent,
        route_weight,
        expert_ids,
        live_tokens[0],
        replica_plan[0],
        slot_count,
        CAP,
    )
    gathered = (
        lax.all_gather(w_gate, "dp", axis=0, tiled=True),
        lax.all_gather(w_up, "dp", axis=0, tiled=True),
        lax.all_gather(w_down, "dp", axis=1, tiled=True),
    )
    full_gate, full_up, full_down = gathered
    recv_tokens, recv_cots = send_rows(token_rows, cot_rows, members)
    own_gate = dequantize(full_gate, scale_gate)
    own_up = dequantize(full_up, scale_up)
    own_down = dequantize(full_down, scale_down)
    leading = expert_terms(
        recv_tokens[:, 0].reshape(-1, width),
        recv_cots[:, 0].reshape(-1, width),
        own_gate,
        own_up,
        own_down,
    )
    trailing = expert_terms(
        recv_tokens[:, 1].reshape(-1, width),
        recv_cots[:, 1].reshape(-1, width),
        own_gate,
        own_up,
        own_down,
    )
    dx_parts = jnp.stack(
        [leading[3].reshape(members, CAP, width), trailing[3].reshape(members, CAP, width)], axis=1
    )
    returned = lax.all_to_all(dx_parts, "expert", split_axis=0, concat_axis=0, tiled=True)
    summed = jnp.sum(returned.astype(jnp.float32).reshape(slot_count, HSH, 2, CAP, width), axis=1)
    sum_gate = (leading[0].astype(jnp.float32) + trailing[0].astype(jnp.float32)).astype(
        jnp.bfloat16
    )
    sum_up = (leading[1].astype(jnp.float32) + trailing[1].astype(jnp.float32)).astype(jnp.bfloat16)
    sum_down = (leading[2].astype(jnp.float32) + trailing[2].astype(jnp.float32)).astype(
        jnp.bfloat16
    )
    stacked = jnp.stack([sum_gate, sum_up, sum_down], axis=0)
    received = lax.all_to_all(stacked, "dp", split_axis=1, concat_axis=0, tiled=True)
    rows_here = received.shape[1]
    totals = jnp.sum(received.astype(jnp.float32).reshape(groups, 3, rows_here, -1), axis=0)
    totals = totals.astype(jnp.bfloat16)
    d_tokens = jnp.dot(flat, summed.reshape(-1, width), precision=lax.Precision.HIGHEST).astype(
        jnp.bfloat16
    )
    return (d_tokens, totals[0], totals[1], totals[2].T)


def solution(mesh):
    return jax.shard_map(
        on_device,
        mesh=mesh,
        in_specs=(
            P(("dp", "expert"), None),
            P(("dp", "expert"), None),
            P(("dp", "expert"), None),
            P(("dp", "expert"), None),
            P(("dp", "expert")),
            P(("dp", "expert"), None),
            P("dp", "expert"),
            P("dp", "expert"),
            P("expert", "dp"),
            P(None, "expert"),
            P(None, "expert"),
            P("expert", None),
        ),
        out_specs=(
            P(("dp", "expert"), None),
            P("dp", "expert"),
            P("dp", "expert"),
            P("expert", "dp"),
        ),
        check_vma=False,
    )
```

profile of v0, /device:TPU:20, one launch (start us, length us, event | category | flops | bytes accessed | tf_op | source)
XLA Modules:
  0.0 513.7 jit_solution(6729519328803929821)
XLA Ops:
  12.1 15.6 %all-to-all-start.1 = ((bf16[32,2,4,3584]{3,2,1,0:T(4,128)(2,1)}), bf16[32,2,4,3584]{3,2,1,0:T(4,128)(2,1)S(1)}, u32[]{:S(2)}, u32[]{:S(2)}) async-start(bf16[32,2,4,3584]{3,2,1,0:T(4,128)(2,1)} %bitcast.102), calls=%async_computation.1 | async-start | bytes 3670016 | tf_op jit(solution)/shard_map/all_to_all | solution.py:76
  29.9 86.5 %all-to-all-done.1 = bf16[32,2,4,3584]{3,2,1,0:T(4,128)(2,1)S(1)} async-done(((bf16[32,2,4,3584]{3,2,1,0:T(4,128)(2,1)}), bf16[32,2,4,3584]{3,2,1,0:T(4,128)(2,1)S(1)}, u32[]{:S(2)}, u32[]{:S(2)}) %all-to-all-start.1) | async-done | bytes 1835040 | tf_op jit(solution)/shard_map/all_to_all | solution.py:76
  116.4 1.8 broadcast_in_dim.56
  118.2 4.9 all-to-all-start
  124.3 3.1 fusion.21
  127.4 25.3 %all-gather.8.cloned.1.call-done = bf16[3584,256]{1,0:T(8,128)(2,1)} async-done(((bf16[224,256]{1,0:T(8,128)(2,1)}), bf16[3584,256]{1,0:T(8,128)(2,1)}) %all-gather.8.cloned.1.call-update) | async-done | bytes 1835024 | tf_op jit(solution)/shard_map/all_gather | solution.py:114
  152.8 8.4 %broadcast_in_dim.64 = f32[3584,2,128]{2,1,0:T(2,128)S(1)} broadcast(f32[3584,2]{1,0:T(8,128)S(1)} %bitcast.103), dimensions={0,1} | broadcast | bytes 3698688 | tf_op jit(solution)/shard_map/broadcast_in_dim | solution.py:13
  161.6 53.3 %all-gather.6.cloned.1.call-done = bf16[3584,256]{1,0:T(8,128)(2,1)} async-done(((bf16[224,256]{1,0:T(8,128)(2,1)}), bf16[3584,256]{1,0:T(8,128)(2,1)}) %all-gather.6.cloned.1.call-update) | async-done | bytes 1835024 | tf_op jit(solution)/shard_map/all_gather | solution.py:115
  215.1 8.2 %broadcast_in_dim.62 = f32[3584,2,128]{2,1,0:T(2,128)S(1)} broadcast(f32[3584,2]{1,0:T(8,128)S(1)} %bitcast.104), dimensions={0,1} | broadcast | bytes 3698688 | tf_op jit(solution)/shard_map/broadcast_in_dim | solution.py:13
  225.0 1.9 fusion.36
  228.5 2.4 reshape_squeeze.13
  234.4 3.3 fusion.35
  237.7 2.4 reshape_squeeze.14
  240.1 2.4 reshape_squeeze.12
  242.5 2.0 fusion.3
  251.0 29.2 %copy.80 = bf16[3,3584,256]{2,0,1:T(4,128)(2,1)} copy(bf16[3,3584,256]{2,1,0:T(8,128)(2,1)S(1)} %pad_maximum_fusion) | data formatting | bytes 11010048 | tf_op jit(solution)/shard_map/stack | solution.py:149
  280.2 7.2 %all-to-all-start.3 = ((bf16[3,3584,256]{2,0,1:T(4,128)(2,1)}), bf16[3,3584,256]{2,0,1:T(4,128)(2,1)}, u32[]{:S(2)}, u32[]{:S(2)}) async-start(bf16[3,3584,256]{2,0,1:T(4,128)(2,1)} %copy.80), calls=%async_computation.3 | async-start | bytes 14680064 | tf_op jit(solution)/shard_map/all_to_all | solution.py:150
  290.6 1.8 stack_reshape.7
  294.8 2.4 pad_maximum_fusion.1
  297.3 105.3 %all-to-all-done.3 = bf16[3,3584,256]{2,0,1:T(4,128)(2,1)} async-done(((bf16[3,3584,256]{2,0,1:T(4,128)(2,1)}), bf16[3,3584,256]{2,0,1:T(4,128)(2,1)}, u32[]{:S(2)}, u32[]{:S(2)}) %all-to-all-start.3) | async-done | bytes 5505056 | tf_op jit(solution)/shard_map/all_to_all | solution.py:150
  402.6 12.9 %all-to-all-start.2 = ((bf16[32,2,4,3584]{3,2,1,0:T(4,128)(2,1)}), bf16[32,2,4,3584]{3,2,1,0:T(4,128)(2,1)S(1)}, u32[]{:S(2)}, u32[]{:S(2)}) async-start(bf16[32,2,4,3584]{3,2,1,0:T(4,128)(2,1)} %pad_maximum_fusion.1), calls=%async_computation.2 | async-start | bytes 3670016 | tf_op jit(solution)/shard_map/all_to_all | solution.py:140
  415.5 6.4 %reduce_sum.42 = bf16[3,224,256]{2,0,1:T(4,128)(2,1)S(1)} reduce(bf16[3,16,224,256]{3,0,2,1:T(4,128)(2,1)} %bitcast.18, bf16[]{:T(256)} %constant.33.clone.1), dimensions={1}, to_apply=%region_5.6 | reduce | flops 2580480 | bytes 5849090 | tf_op jit(solution)/shard_map/reduce_sum | solution.py:152
  424.4 80.0 %all-to-all-done.2 = bf16[32,2,4,3584]{3,2,1,0:T(4,128)(2,1)S(1)} async-done(((bf16[32,2,4,3584]{3,2,1,0:T(4,128)(2,1)}), bf16[32,2,4,3584]{3,2,1,0:T(4,128)(2,1)S(1)}, u32[]{:S(2)}, u32[]{:S(2)}) %all-to-all-start.2) | async-done | bytes 1835040 | tf_op jit(solution)/shard_map/all_to_all | solution.py:140
  505.2 1.9 fusion.15
  (102 shorter events, 30.2 us)
Async XLA Ops:
  7.2 2.8 copy-start
  12.1 17.1 %copy-start.15 = (s32[128,8]{0,1:T(8,128)S(1)}, s32[128,8]{0,1:T(8,128)}, u32[]{:S(2)}) copy-start(s32[128,8]{0,1:T(8,128)} %param.15) | copy-start | bytes 12292
  12.1 17.1 %copy-start.16 = (f32[128,8]{0,1:T(8,128)S(1)}, f32[128,8]{0,1:T(8,128)}, u32[]{:S(2)}) copy-start(f32[128,8]{0,1:T(8,128)} %param.14) | copy-start | bytes 12292
  12.1 17.3 %copy-start.14 = (bf16[128,3584]{1,0:T(8,128)(2,1)S(1)}, bf16[128,3584]{1,0:T(8,128)(2,1)}, u32[]{:S(2)}) copy-start(bf16[128,3584]{1,0:T(8,128)(2,1)} %param.13) | copy-start | bytes 2752516
  12.1 104.2 %all-to-all-start.1 = ((bf16[32,2,4,3584]{3,2,1,0:T(4,128)(2,1)}), bf16[32,2,4,3584]{3,2,1,0:T(4,128)(2,1)S(1)}, u32[]{:S(2)}, u32[]{:S(2)}) async-start(bf16[32,2,4,3584]{3,2,1,0:T(4,128)(2,1)} %bitcast.102), calls=%async_computation.1 | async-start | bytes 3670016 | tf_op jit(solution)/shard_map/all_to_all | solution.py:76
  27.8 96.5 %all-gather.4.cloned.1.call-start = ((), (), s32[]{:S(2)}) async-start(), calls=%async_computation.4 | async-start | bytes 1949696 | tf_op jit(solution)/shard_map/all_gather | solution.py:116
  28.5 124.2 %all-gather.8.cloned.1.call-start = ((), (), s32[]{:S(2)}) async-start(), calls=%async_computation.6 | async-start | bytes 1949696 | tf_op jit(solution)/shard_map/all_gather | solution.py:114
  116.4 1.8 copy-start.7
  118.2 5.6 %copy-start.17 = (f32[28,2]{0,1:T(2,128)S(1)}, f32[28,2]{0,1:T(2,128)}, u32[]{:S(2)}) copy-start(f32[28,2]{0,1:T(2,128)} %param.21) | copy-start | bytes 676
  118.2 5.7 %copy-start.18 = (f32[28,2]{0,1:T(2,128)S(1)}, f32[28,2]{0,1:T(2,128)}, u32[]{:S(2)}) copy-start(f32[28,2]{0,1:T(2,128)} %param.22) | copy-start | bytes 676
  118.2 5.8 %copy-start.19 = (f32[2,28]{1,0:T(2,128)S(1)}, f32[2,28]{1,0:T(2,128)}, u32[]{:S(2)}) copy-start(f32[2,28]{1,0:T(2,128)} %param.23) | copy-start | bytes 676
  118.2 116.2 %all-to-all-start = ((bf16[32,2,4,3584]{3,2,1,0:T(4,128)(2,1)}), bf16[32,2,4,3584]{3,2,1,0:T(4,128)(2,1)}, u32[]{:S(2)}, u32[]{:S(2)}) async-start(bf16[32,2,4,3584]{3,2,1,0:T(4,128)(2,1)} %bitcast.101), calls=%async_computation | async-start | bytes 3670016 | tf_op jit(solution)/shard_map/all_to_all | solution.py:79
  123.1 91.9 %all-gather.6.cloned.1.call-start = ((), (), s32[]{:S(2)}) async-start(), calls=%async_computation.5 | async-start | bytes 1949696 | tf_op jit(solution)/shard_map/all_gather | solution.py:115
  152.8 8.4 %copy-start.11 = (bf16[3584,256]{1,0:T(8,128)(2,1)S(1)}, bf16[3584,256]{1,0:T(8,128)(2,1)}, u32[]{:S(2)}) copy-start(bf16[3584,256]{1,0:T(8,128)(2,1)} %all-gather.8.cloned.1.call-done) | copy-start | bytes 5505028
  215.1 8.2 %copy-start.12 = (bf16[3584,256]{1,0:T(8,128)(2,1)S(1)}, bf16[3584,256]{1,0:T(8,128)(2,1)}, u32[]{:S(2)}) copy-start(bf16[3584,256]{1,0:T(8,128)(2,1)} %all-gather.6.cloned.1.call-done) | copy-start | bytes 5505028
  223.3 1.7 copy-start.8
  230.9 1.5 copy-start.2
  242.5 2.0 copy-start.10
  242.5 2.1 copy-start.13
  280.2 122.4 %all-to-all-start.3 = ((bf16[3,3584,256]{2,0,1:T(4,128)(2,1)}), bf16[3,3584,256]{2,0,1:T(4,128)(2,1)}, u32[]{:S(2)}, u32[]{:S(2)}) async-start(bf16[3,3584,256]{2,0,1:T(4,128)(2,1)} %copy.80), calls=%async_computation.3 | async-start | bytes 14680064 | tf_op jit(solution)/shard_map/all_to_all | solution.py:150
  287.4 1.5 copy-start.3
  292.4 1.5 copy-start.4
  402.6 101.8 %all-to-all-start.2 = ((bf16[32,2,4,3584]{3,2,1,0:T(4,128)(2,1)}), bf16[32,2,4,3584]{3,2,1,0:T(4,128)(2,1)S(1)}, u32[]{:S(2)}, u32[]{:S(2)}) async-start(bf16[32,2,4,3584]{3,2,1,0:T(4,128)(2,1)} %pad_maximum_fusion.1), calls=%async_computation.2 | async-start | bytes 3670016 | tf_op jit(solution)/shard_map/all_to_all | solution.py:140
  504.4 2.7 copy-start.1
  (3 other events, 3.5 us)
Sparse Core Ops, SparseCore 0:
  31.6 58.7 all-gather.3
  93.5 59.1 all-gather.7
  155.7 59.1 all-gather.5
where the time goes:
time: 515 us; the launch traced here: 514 us
  waiting for transfers between devices  353 us (69%)
  local copies, waits for them, and re-layouts  73.9 us (14%)
  starting transfers between devices  40.7 us (8%)
  other arithmetic  17.5 us (3%)
  between operations  14.8 us (3%)
  matrix products  14.2 us (3%)
    all_to_all x1, waiting for transfers between devices, on_device(): lax.all_to_all(stacked, 'dp', split_axis=1, concat_axis=0, tiled=True)  105 us
    all_to_all x1, waiting for transfers between devices, send_rows(): lax.all_to_all(fan_out(token_rows, members), 'expert', split_axis=0, conc...  86.5 us
    all_to_all x1, waiting for transfers between devices, on_device(): lax.all_to_all(dx_parts, 'expert', split_axis=0, concat_axis=0, tiled=True)  80 us
    all_gather x1, waiting for transfers between devices, on_device(): lax.all_gather(w_up, 'dp', axis=0, tiled=True)  53.3 us
    another operation x1, local copies, waits for them, and re-layouts, on_device(): stacked = jnp.stack([sum_gate, sum_up, sum_down], axis=0)  29.2 us
    all_gather x1, waiting for transfers between devices, on_device(): lax.all_gather(w_gate, 'dp', axis=0, tiled=True)  25.3 us
    broadcast_in_dim x2, local copies, waits for them, and re-layouts, dequantize(): jnp.repeat(jnp.repeat(scale, block_rows, axis=0), block_cols, axis=1)  16.6 us
    all_to_all x1, starting transfers between devices, send_rows(): lax.all_to_all(fan_out(token_rows, members), 'expert', split_axis=0, conc...  15.6 us
  transfers between devices with their start and end apart: 7, of which 5 were waited for; matrix products, arithmetic and copies ran while one was open for 10% of the time, Pallas kernels for 0%

commit v1 on v0

--- a/solution.py
+++ b/solution.py
@@ -110,9 +110,22 @@
         slot_count,
         CAP,
     )
+
+    def find_set_on(state, shard_axis):
+        k_now = jnp.concatenate(
+            lax.all_to_all(
+                jnp.stack(lax.axis_size(shard_axis) * [state]),
+                axis_name=shard_axis,
+                split_axis=0,
+                concat_axis=0,
+            ),
+            0,
+        )
+        return k_now
+
     gathered = (
         lax.all_gather(w_gate, "dp", axis=0, tiled=True),
-        lax.all_gather(w_up, "dp", axis=0, tiled=True),
+        find_set_on(w_up, "dp"),
         lax.all_gather(w_down, "dp", axis=1, tiled=True),
     )
     full_gate, full_up, full_down = gathered

time: 515 us -> 531 us (1.031)
  starting transfers between devices: 40.7 us -> 55.3 us
  waiting for transfers between devices: 353 us -> 339 us
  other arithmetic: 17.5 us -> 24.6 us
  local copies, waits for them, and re-layouts: 73.9 us -> 80.9 us
    all_gather x1 -> x0, waiting for transfers between devices: 53.3 us -> none  [on_device(): lax.all_gather(w_up, 'dp', axis=0, tiled=True)]
    all_to_all x0 -> x1, waiting for transfers between devices: none -> 19.8 us  [find_set_on(): lax.all_to_all(jnp.stack(lax.axis_size(shard_axis) * [state]), axis_name=...]
    all_gather x1, waiting for transfers between devices: 25.3 us -> 43.4 us  [on_device(): lax.all_gather(w_gate, 'dp', axis=0, tiled=True)]
    all_to_all x1, waiting for transfers between devices: 0.01 us -> 9.45 us  [send_rows(): lax.all_to_all(fan_out(cot_rows, members), 'expert', split_axis=0, concat...]
    all_to_all x0 -> x1, starting transfers between devices: none -> 9.32 us  [find_set_on(): lax.all_to_all(jnp.stack(lax.axis_size(shard_axis) * [state]), axis_name=...]
    convert_element_type x3 -> x4, other arithmetic: 5.2 us -> 13.9 us  [dequantize(): return (values.astype(jnp.float32) * spread).astype(jnp.bfloat16)]
    all_to_all x1, waiting for transfers between devices: 105 us -> 98.4 us  [on_device(): lax.all_to_all(stacked, 'dp', split_axis=1, concat_axis=0, tiled=True)]
  transfers between devices with their start and end apart: 7 -> 7, of which waited for: 5 -> 6; matrix products, arithmetic and copies ran while one was open for 10% -> 12% of each run, Pallas kernels for 0% -> 0%
where the time goes in v1:
time: 531 us; the launch traced here: 529 us
  waiting for transfers between devices  339 us (64%)
  local copies, waits for them, and re-layouts  80.9 us (15%)
  starting transfers between devices  55.3 us (10%)
  other arithmetic  24.6 us (5%)
  between operations  15.1 us (3%)
  matrix products  14.2 us (3%)
    all_to_all x1, waiting for transfers between devices, on_device(): lax.all_to_all(stacked, 'dp', split_axis=1, concat_axis=0, tiled=True)  98.4 us
    all_to_all x1, waiting for transfers between devices, send_rows(): lax.all_to_all(fan_out(token_rows, members), 'expert', split_axis=0, conc...  87.3 us
    all_to_all x1, waiting for transfers between devices, on_device(): lax.all_to_all(dx_parts, 'expert', split_axis=0, concat_axis=0, tiled=True)  79.8 us
    all_gather x1, waiting for transfers between devices, on_device(): lax.all_gather(w_gate, 'dp', axis=0, tiled=True)  43.4 us
    another operation x1, local copies, waits for them, and re-layouts, on_device(): stacked = jnp.stack([sum_gate, sum_up, sum_down], axis=0)  29.3 us
    all_to_all x1, waiting for transfers between devices, find_set_on(): lax.all_to_all(jnp.stack(lax.axis_size(shard_axis) * [state]), axis_name=...  19.8 us
    all_to_all x1, starting transfers between devices, on_device(): lax.all_to_all(dx_parts, 'expert', split_axis=0, concat_axis=0, tiled=True)  17 us
    broadcast_in_dim x2, local copies, waits for them, and re-layouts, dequantize(): jnp.repeat(jnp.repeat(scale, block_rows, axis=0), block_cols, axis=1)  16.6 us
  transfers between devices with their start and end apart: 7, of which 6 were waited for; matrix products, arithmetic and copies ran while one was open for 12% of the time, Pallas kernels for 0%

profile of v1, /device:TPU:20, one launch (start us, length us, event | category | flops | bytes accessed | tf_op | source)
XLA Modules:
  0.0 529.4 jit_solution(14580718175447703445)
XLA Ops:
  7.2 2.4 stack.15
  9.6 9.3 %all-to-all-start.2 = ((bf16[16,224,256]{2,1,0:T(8,128)(2,1)}), bf16[16,224,256]{2,1,0:T(8,128)(2,1)S(1)}, u32[]{:S(2)}, u32[]{:S(2)}) async-start(bf16[16,224,256]{2,1,0:T(8,128)(2,1)} %stack.15), calls=%async_computation.2 | async-start | bytes 3670016 | tf_op jit(solution)/shard_map/all_to_all | solution.py:116
  20.7 19.8 %all-to-all-done.2 = bf16[16,224,256]{2,1,0:T(8,128)(2,1)S(1)} async-done(((bf16[16,224,256]{2,1,0:T(8,128)(2,1)}), bf16[16,224,256]{2,1,0:T(8,128)(2,1)S(1)}, u32[]{:S(2)}, u32[]{:S(2)}) %all-to-all-start.2) | async-done | bytes 1835040 | tf_op jit(solution)/shard_map/all_to_all | solution.py:116
  42.3 15.9 %all-to-all-start.1 = ((bf16[32,2,4,3584]{3,2,1,0:T(4,128)(2,1)}), bf16[32,2,4,3584]{3,2,1,0:T(4,128)(2,1)}, u32[]{:S(2)}, u32[]{:S(2)}) async-start(bf16[32,2,4,3584]{3,2,1,0:T(4,128)(2,1)} %bitcast.109), calls=%async_computation.1 | async-start | bytes 3670016 | tf_op jit(solution)/shard_map/all_to_all | solution.py:76
  59.6 87.3 %all-to-all-done.1 = bf16[32,2,4,3584]{3,2,1,0:T(4,128)(2,1)} async-done(((bf16[32,2,4,3584]{3,2,1,0:T(4,128)(2,1)}), bf16[32,2,4,3584]{3,2,1,0:T(4,128)(2,1)}, u32[]{:S(2)}, u32[]{:S(2)}) %all-to-all-start.1) | async-done | bytes 1835040 | tf_op jit(solution)/shard_map/all_to_all | solution.py:76
  148.7 4.9 all-to-all-start
  156.7 3.0 reshape.373
  159.7 9.9 %multiply_convert_fusion = bf16[3584,2,128]{2,1,0:T(2,128)(2,1)} fusion(f32[3584,2,128]{2,1,0:T(2,128)} %reshape.373, f32[3584,2]{1,0:T(8,128)} %copy.86), kind=kLoop, calls=%fused_computation.38 | loop fusion | flops 1835008 | bytes 5533696 | tf_op jit(solution)/shard_map/convert_element_type | solution.py:14
  169.7 3.1 fusion.21
  172.8 43.4 %all-gather.5.cloned.1.call-done = bf16[3584,256]{1,0:T(8,128)(2,1)} async-done(((bf16[224,256]{1,0:T(8,128)(2,1)}), bf16[3584,256]{1,0:T(8,128)(2,1)}) %all-gather.5.cloned.1.call-update) | async-done | bytes 1835024 | tf_op jit(solution)/shard_map/all_gather | solution.py:127
  216.3 8.2 %broadcast_in_dim.64 = f32[3584,2,128]{2,1,0:T(2,128)S(1)} broadcast(f32[3584,2]{1,0:T(8,128)S(1)} %bitcast.110), dimensions={0,1} | broadcast | bytes 3698688 | tf_op jit(solution)/shard_map/broadcast_in_dim | solution.py:13
  224.9 3.0 fusion.42
  234.3 9.5 %all-to-all-done = bf16[32,2,4,3584]{3,2,1,0:T(4,128)(2,1)} async-done(((bf16[32,2,4,3584]{3,2,1,0:T(4,128)(2,1)}), bf16[32,2,4,3584]{3,2,1,0:T(4,128)(2,1)}, u32[]{:S(2)}, u32[]{:S(2)}) %all-to-all-start) | async-done | bytes 1835040 | tf_op jit(solution)/shard_map/all_to_all | solution.py:79
  243.7 3.3 fusion.41
  247.1 2.4 reshape_squeeze.12
  249.4 2.4 reshape_squeeze.14
  260.0 29.3 %copy.92 = bf16[3,3584,256]{2,0,1:T(4,128)(2,1)} copy(bf16[3,3584,256]{2,1,0:T(8,128)(2,1)S(1)} %pad_maximum_fusion) | data formatting | bytes 11010048 | tf_op jit(solution)/shard_map/stack | solution.py:162
  289.3 8.1 %all-to-all-start.4 = ((bf16[3,3584,256]{2,0,1:T(4,128)(2,1)}), bf16[3,3584,256]{2,0,1:T(4,128)(2,1)}, u32[]{:S(2)}, u32[]{:S(2)}) async-start(bf16[3,3584,256]{2,0,1:T(4,128)(2,1)} %copy.92), calls=%async_computation.4 | async-start | bytes 14680064 | tf_op jit(solution)/shard_map/all_to_all | solution.py:163
  297.4 8.4 %broadcast_in_dim.62 = f32[3584,2,128]{2,1,0:T(2,128)S(1)} broadcast(f32[3584,2]{1,0:T(8,128)} %copy.86), dimensions={0,1} | broadcast | bytes 3698688 | tf_op jit(solution)/shard_map/broadcast_in_dim | solution.py:13
  313.4 2.4 pad_maximum_fusion.1
  315.8 98.4 %all-to-all-done.4 = bf16[3,3584,256]{2,0,1:T(4,128)(2,1)} async-done(((bf16[3,3584,256]{2,0,1:T(4,128)(2,1)}), bf16[3,3584,256]{2,0,1:T(4,128)(2,1)}, u32[]{:S(2)}, u32[]{:S(2)}) %all-to-all-start.4) | async-done | bytes 5505056 | tf_op jit(solution)/shard_map/all_to_all | solution.py:163
  414.2 17.0 %all-to-all-start.3 = ((bf16[32,2,4,3584]{3,2,1,0:T(4,128)(2,1)}), bf16[32,2,4,3584]{3,2,1,0:T(4,128)(2,1)S(1)}, u32[]{:S(2)}, u32[]{:S(2)}) async-start(bf16[32,2,4,3584]{3,2,1,0:T(4,128)(2,1)} %pad_maximum_fusion.1), calls=%async_computation.3 | async-start | bytes 3670016 | tf_op jit(solution)/shard_map/all_to_all | solution.py:153
  431.2 6.4 %reduce_sum.42 = bf16[3,224,256]{2,0,1:T(4,128)(2,1)S(1)} reduce(bf16[3,16,224,256]{3,0,2,1:T(4,128)(2,1)} %bitcast.19, bf16[]{:T(256)} %constant.33.clone.1), dimensions={1}, to_apply=%region_5.6 | reduce | flops 2580480 | bytes 5849090 | tf_op jit(solution)/shard_map/reduce_sum | solution.py:165
  440.0 79.8 %all-to-all-done.3 = bf16[32,2,4,3584]{3,2,1,0:T(4,128)(2,1)S(1)} async-done(((bf16[32,2,4,3584]{3,2,1,0:T(4,128)(2,1)}), bf16[32,2,4,3584]{3,2,1,0:T(4,128)(2,1)S(1)}, u32[]{:S(2)}, u32[]{:S(2)}) %all-to-all-start.3) | async-done | bytes 1835040 | tf_op jit(solution)/shard_map/all_to_all | solution.py:153
  (105 shorter events, 36.9 us)
Async XLA Ops:
  7.2 13.1 %copy-start = (bf16[128,3584]{1,0:T(8,128)(2,1)S(1)}, bf16[128,3584]{1,0:T(8,128)(2,1)}, u32[]{:S(2)}) copy-start(bf16[128,3584]{1,0:T(8,128)(2,1)} %param.12) | copy-start | bytes 2752516
  9.6 10.1 %copy-start.14 = (s32[128,8]{0,1:T(8,128)S(1)}, s32[128,8]{0,1:T(8,128)}, u32[]{:S(2)}) copy-start(s32[128,8]{0,1:T(8,128)} %param.15) | copy-start | bytes 12292
  9.6 10.1 %copy-start.19 = (s32[1,4]{1,0:T(1,128)S(1)}, s32[1,4]{1,0:T(1,128)}, u32[]{:S(2)}) copy-start(s32[1,4]{1,0:T(1,128)} %param.17) | copy-start | bytes 52
  9.6 30.8 %all-to-all-start.2 = ((bf16[16,224,256]{2,1,0:T(8,128)(2,1)}), bf16[16,224,256]{2,1,0:T(8,128)(2,1)S(1)}, u32[]{:S(2)}, u32[]{:S(2)}) async-start(bf16[16,224,256]{2,1,0:T(8,128)(2,1)} %stack.15), calls=%async_computation.2 | async-start | bytes 3670016 | tf_op jit(solution)/shard_map/all_to_all | solution.py:116
  40.4 116.3 %copy-start.4 = (bf16[16,224,256]{2,1,0:T(8,128)(2,1)}, bf16[16,224,256]{2,1,0:T(8,128)(2,1)S(1)}, u32[]{:S(2)}) copy-start(bf16[16,224,256]{2,1,0:T(8,128)(2,1)S(1)} %all-to-all-done.2) | copy-start | bytes 5505028
  42.3 16.6 %copy-start.15 = (f32[128,8]{0,1:T(8,128)S(1)}, f32[128,8]{0,1:T(8,128)}, u32[]{:S(2)}) copy-start(f32[128,8]{0,1:T(8,128)} %param.14) | copy-start | bytes 12292
  42.3 16.8 %copy-start.13 = (bf16[128,3584]{1,0:T(8,128)(2,1)S(1)}, bf16[128,3584]{1,0:T(8,128)(2,1)}, u32[]{:S(2)}) copy-start(bf16[128,3584]{1,0:T(8,128)(2,1)} %param.13) | copy-start | bytes 2752516
  42.3 104.5 %all-to-all-start.1 = ((bf16[32,2,4,3584]{3,2,1,0:T(4,128)(2,1)}), bf16[32,2,4,3584]{3,2,1,0:T(4,128)(2,1)}, u32[]{:S(2)}, u32[]{:S(2)}) async-start(bf16[32,2,4,3584]{3,2,1,0:T(4,128)(2,1)} %bitcast.109), calls=%async_computation.1 | async-start | bytes 3670016 | tf_op jit(solution)/shard_map/all_to_all | solution.py:76
  58.2 111.4 %all-gather.3.cloned.1.call-start = ((), (), s32[]{:S(2)}) async-start(), calls=%async_computation.5 | async-start | bytes 1949696 | tf_op jit(solution)/shard_map/all_gather | solution.py:129
  148.7 5.6 %copy-start.16 = (f32[28,2]{0,1:T(2,128)S(1)}, f32[28,2]{0,1:T(2,128)}, u32[]{:S(2)}) copy-start(f32[28,2]{0,1:T(2,128)} %param.21) | copy-start | bytes 676
  148.7 5.7 %copy-start.17 = (f32[28,2]{0,1:T(2,128)S(1)}, f32[28,2]{0,1:T(2,128)}, u32[]{:S(2)}) copy-start(f32[28,2]{0,1:T(2,128)} %param.22) | copy-start | bytes 676
  148.7 5.8 %copy-start.18 = (f32[2,28]{1,0:T(2,128)S(1)}, f32[2,28]{1,0:T(2,128)}, u32[]{:S(2)}) copy-start(f32[2,28]{1,0:T(2,128)} %param.23) | copy-start | bytes 676
  148.7 95.1 %all-to-all-start = ((bf16[32,2,4,3584]{3,2,1,0:T(4,128)(2,1)}), bf16[32,2,4,3584]{3,2,1,0:T(4,128)(2,1)}, u32[]{:S(2)}, u32[]{:S(2)}) async-start(bf16[32,2,4,3584]{3,2,1,0:T(4,128)(2,1)} %bitcast.108), calls=%async_computation | async-start | bytes 3670016 | tf_op jit(solution)/shard_map/all_to_all | solution.py:79
  153.6 62.6 %all-gather.5.cloned.1.call-start = ((), (), s32[]{:S(2)}) async-start(), calls=%async_computation.6 | async-start | bytes 1949696 | tf_op jit(solution)/shard_map/all_gather | solution.py:127
  216.3 8.2 %copy-start.10 = (bf16[3584,256]{1,0:T(8,128)(2,1)S(1)}, bf16[3584,256]{1,0:T(8,128)(2,1)}, u32[]{:S(2)}) copy-start(bf16[3584,256]{1,0:T(8,128)(2,1)} %all-gather.5.cloned.1.call-done) | copy-start | bytes 5505028
  232.0 1.5 copy-start.11
  251.8 2.0 copy-start.9
  251.8 2.1 copy-start.12
  289.3 124.9 %all-to-all-start.4 = ((bf16[3,3584,256]{2,0,1:T(4,128)(2,1)}), bf16[3,3584,256]{2,0,1:T(4,128)(2,1)}, u32[]{:S(2)}, u32[]{:S(2)}) async-start(bf16[3,3584,256]{2,0,1:T(4,128)(2,1)} %copy.92), calls=%async_computation.4 | async-start | bytes 14680064 | tf_op jit(solution)/shard_map/all_to_all | solution.py:163
  297.4 8.4 %copy-start.5 = (bf16[16,224,256]{2,1,0:T(8,128)(2,1)S(1)}, bf16[16,224,256]{2,1,0:T(8,128)(2,1)}, u32[]{:S(2)}) copy-start(bf16[16,224,256]{2,1,0:T(8,128)(2,1)} %copy-done.4) | copy-start | bytes 5505028
  306.2 1.2 copy-start.2
  310.9 1.5 copy-start.3
  414.2 105.6 %all-to-all-start.3 = ((bf16[32,2,4,3584]{3,2,1,0:T(4,128)(2,1)}), bf16[32,2,4,3584]{3,2,1,0:T(4,128)(2,1)S(1)}, u32[]{:S(2)}, u32[]{:S(2)}) async-start(bf16[32,2,4,3584]{3,2,1,0:T(4,128)(2,1)} %pad_maximum_fusion.1), calls=%async_computation.3 | async-start | bytes 3670016 | tf_op jit(solution)/shard_map/all_to_all | solution.py:153
  519.8 2.7 copy-start.1
  (3 other events, 3.5 us)
Sparse Core Ops, SparseCore 0:
  62.1 58.6 all-gather.2
  157.4 58.6 all-gather.4
